TPU v7x, 256 devices: a whole 4x4x8 slice. The times are simulated.
256 devices in a mesh: ka: 16 (over x, z_hi), row: 16 (over z_lo, y, core).
Axes of the slice: x: 4, y: 4, z: 8 (z_hi: 4, z_lo: 2; z = z_hi * 2 + z_lo), core: 2. Of those that a mesh axis runs over, the one named last changes fastest.
Arguments:
- gauge: bfloat16 [256, 2, 384, 384], P(('ka', 'row')), may hold values from -3 to 3
- energies: float32 [256, 384], P(('ka', 'row')), may hold values from -5 to 5
- kmesh: int32 [3, 256], replicated, may hold values from 0 to 11
- lattice: int32 [3, 1024], P(None, 'row'), may hold values from -8 to 8
- degeneracy: int32 [1024], P('row'), may hold values from 1 to 8
- path: int32 [3, 32], replicated, may hold values from 0 to 63
Outputs:
- lattice_h: bfloat16 [1024, 384, 768], P('row', 'ka')
- path_h: float32 [32, 384, 768], P('row', 'ka')
All inputs are finite; a program needn't handle non-finite values.
Results may differ from a plain program's by a relative error of at most 0.006.
Values may be sent and summed in bfloat16 or wider, within the bound.
A program may use at most 64 MiB of HBM per device.

v0:
```python
import math

import jax
import jax.numpy as jnp
from jax import lax
from jax.sharding import PartitionSpec as P

MESH = 12
PATH_DEN = 64


def in_order(pieces, dim):
    shape = list(pieces.shape[1:])
    shape[dim] *= pieces.shape[0]
    return jnp.moveaxis(pieces, 0, dim).reshape(shape)


def gather_together(arrays, axis, dims):
    vector = jnp.concatenate([a.reshape(-1) for a in arrays])
    lines, at, done = (lax.all_gather(vector, axis), 0, [])
    for a, dim in zip(arrays, dims):
        pieces = lines[:, at : at + a.size].reshape(-1, *a.shape)
        done.append(in_order(pieces, dim))
        at += a.size
    return tuple(done)


def phases(vectors, coords):
    windings = jnp.mod(jnp.sum(vectors[:, :, None] * coords[:, None, :], 0), MESH)
    angles = windings.astype(jnp.float32) * (2.0 * math.pi / MESH)
    return jnp.concatenate([jnp.cos(angles), jnp.sin(angles)], 0).astype(jnp.bfloat16)


def path_factors(path_coords, vectors, counts):
    windings = jnp.mod(jnp.sum(path_coords[:, :, None] * vectors[:, None, :], 0), PATH_DEN)
    angles = windings.astype(jnp.float32) * (2.0 * math.pi / PATH_DEN)
    weights = 1.0 / counts.astype(jnp.float32)
    return jnp.concatenate(
        [jnp.cos(angles) * weights[None, :], jnp.sin(angles) * weights[None, :]], 0
    ).astype(jnp.bfloat16)


def combine_fourier(products, scale_by):
    real_part = products[0, :, :, 0] + products[1, :, :, 1]
    imag_part = products[0, :, :, 1] - products[1, :, :, 0]
    return jnp.concatenate([real_part, imag_part], -1) / scale_by


def combine_path(products):
    real_part = products[0, :, :, 0] - products[1, :, :, 1]
    imag_part = products[0, :, :, 1] + products[1, :, :, 0]
    return jnp.concatenate([real_part, imag_part], -1)


def local(gauge, energies, kmesh, lattice, degeneracy, path):
    per_device = gauge.shape[0]
    orbitals = gauge.shape[2]
    ka_count = lax.axis_size("ka")
    row_count = lax.axis_size("row")
    k_total = kmesh.shape[1]
    path_dev = path.shape[1] // row_count
    scaled = (energies[:, None, :, None] * gauge.astype(jnp.float32)).astype(jnp.bfloat16)
    stacked = jnp.concatenate([gauge[:, 0], gauge[:, 1]], 1)
    partner = jnp.concatenate(
        [
            jnp.concatenate([scaled[:, 0], scaled[:, 1]], 2),
            jnp.concatenate([scaled[:, 1], -scaled[:, 0]], 2),
        ],
        1,
    )
    rotated = jnp.einsum(
        "kna,knb->kab", stacked, partner, preferred_element_type=jnp.float32
    ).astype(jnp.bfloat16)
    arrived = lax.all_to_all(rotated, "ka", split_axis=1, concat_axis=0, tiled=True)
    local_rows = arrived.shape[1]
    lattice_rows = lattice.shape[1]
    k_order = (
        kmesh.reshape(3, ka_count, row_count, per_device).transpose(0, 2, 1, 3).reshape(3, k_total)
    )
    vectors_all, counts_all = gather_together((lattice, degeneracy), "row", (1, 0))
    total_vectors = vectors_all.shape[1]
    own_path = lax.dynamic_slice_in_dim(path, lax.axis_index("row") * path_dev, path_dev, 1)
    factors_path = path_factors(own_path, vectors_all, counts_all).astype(jnp.float32)
    factors_mesh = phases(vectors_all, k_order).astype(jnp.float32)
    with_cos = jnp.dot(
        factors_path,
        factors_mesh[:total_vectors],
        preferred_element_type=jnp.float32,
        precision=lax.Precision.HIGHEST,
    )
    with_sin = jnp.dot(
        factors_path,
        factors_mesh[total_vectors:],
        preferred_element_type=jnp.float32,
        precision=lax.Precision.HIGHEST,
    )
    mixing_real = (with_cos[:path_dev] + with_sin[path_dev:]) / k_total
    mixing_imag = (with_cos[path_dev:] - with_sin[:path_dev]) / k_total
    mixing = jnp.concatenate([mixing_real, mixing_imag], 0)
    k_piece = lax.all_gather(arrived, "row", axis=0, tiled=True)
    amount = k_piece.shape[0]
    fourier_amount = k_piece.shape[0]
    factors = phases(lattice, k_order)
    fourier_sum = jnp.dot(
        factors, k_piece.reshape(fourier_amount, -1), preferred_element_type=jnp.float32
    )
    path_sum = jnp.dot(
        mixing,
        k_piece.reshape(amount, -1).astype(jnp.float32),
        preferred_element_type=jnp.float32,
        precision=lax.Precision.HIGHEST,
    )
    summed, path_sum = (fourier_sum, path_sum)
    products = summed.reshape(2, lattice_rows, local_rows, 2, orbitals)
    lattice_f = combine_fourier(products, k_total)
    path_h = combine_path(path_sum.reshape(2, path_dev, local_rows, 2, orbitals))
    lattice_h = lattice_f.astype(jnp.bfloat16)
    return (lattice_h, path_h)


def solution(mesh):
    return jax.shard_map(
        local,
        mesh=mesh,
        in_specs=(
            P(("ka", "row"), None, None, None),
            P(("ka", "row"), None),
            P(),
            P(None, "row"),
            P("row"),
            P(),
        ),
        out_specs=(P("row", "ka", None), P("row", "ka", None)),
        check_vma=False,
    )
```

profile of v0, /device:TPU:1, one launch (start us, length us, event | category | flops | bytes accessed | tf_op | source)
XLA Modules:
  0.0 144.0 jit_solution(3679040499282533546)
XLA Ops:
  7.2 0.0 copy-start
  7.2 0.0 all-gather.4.cloned.1.call-start
  7.2 0.7 reduce
  7.9 1.2 multiply_convert_fusion
  9.2 1.3 slice_bitcast_fusion.3
  10.5 0.7 fusion.4
  11.1 0.9 copy.74
  12.0 0.5 broadcast.32
  12.6 4.4 %reduce.1 = bf16[384,768]{1,0:T(8,128)(2,1)S(1)} reduce(bf16[384,1,768]{2,1,0:T(2,128)(2,1)S(1)} %bitcast.82, bf16[]{:T(256)} %broadcast.32), dimensions={1}, to_apply=%bitcast.78.reduce_sub_computation | reduce | bytes 1179650
  16.9 0.2 reshape.91
  17.1 29.0 %all_to_all.12 = bf16[16,2,9216]{2,1,0:T(2,128)(2,1)S(1)} all-to-all(bf16[16,2,9216]{2,1,0:T(2,128)(2,1)S(1)} %reshape.91), channel_id=1, replica_groups=mesh['ka'=16,'row'=16] {'ka'}, dimensions={0} | all-to-all | bytes 1179648 | tf_op jit(solution)/shard_map/all_to_all | solution.py:74
  46.1 0.5 reshape.92
  46.6 0.9 copy.65
  47.5 0.0 all-gather.4.cloned.1.call-update
  47.5 0.0 copy-done.2
  47.5 0.1 reshape.80
  47.6 0.0 copy-done.4
  47.6 0.1 pad_add_fusion
  47.7 23.4 %all-gather.1 = s32[16,1,256]{2,1,0:T(1,128)S(1)} all-gather(s32[1,1,256]{2,1,0:T(1,128)S(1)} %bitcast.90), channel_id=2, replica_groups=mesh['ka'=16,'row'=16] {'row'}, dimensions={0}, use_global_device_ids=true | all-gather | bytes 17408 | tf_op jit(solution)/shard_map/all_gather | solution.py:20
  71.1 0.1 reshape.81
  71.2 0.1 mul.99
  71.3 0.1 fusion.25
  71.4 0.1 div.29
  71.5 0.0 copy-done.3
  71.5 0.1 reshape.76
  71.5 0.1 copy.52
  71.6 0.1 mul.89
  71.7 0.0 copy-done
  71.7 0.1 constant_dynamic-slice_fusion
  71.8 0.1 multiply_reduce_fusion.2
  71.9 0.6 multiply_reduce_fusion
  72.5 0.1 multiply_convert_fusion.2
  72.7 0.1 multiply_convert_fusion.1
  72.8 4.5 %fusion.15 = f32[4,256]{1,0:T(4,128)S(1)} fusion(s32[1024,256]{1,0:T(8,128)S(1)} %multiply_reduce_fusion, bf16[2,1024]{1,0:T(2,128)(2,1)S(1)} %multiply_convert_fusion.1, bf16[2,1024]{1,0:T(2,128)(2,1)S(1)} %get-tuple-element.14), kind=kOutput, calls=%fused_computation.27 | convolution fusion | flops 4472832 | bytes 1060864 | tf_op jit(solution)/shard_map/dot_general | solution.py:85
  77.3 4.5 %fusion.16 = f32[4,256]{1,0:T(4,128)S(1)} fusion(s32[1024,256]{1,0:T(8,128)S(1)} %multiply_reduce_fusion, bf16[2,1024]{1,0:T(2,128)(2,1)S(1)} %multiply_convert_fusion.1, bf16[2,1024]{1,0:T(2,128)(2,1)S(1)} %get-tuple-element.14), kind=kOutput, calls=%fused_computation.28 | convolution fusion | flops 4472832 | bytes 1060864 | tf_op jit(solution)/shard_map/dot_general | solution.py:91
  81.8 0.1 multiply_reduce_fusion.1
  81.9 0.3 cosine_convert_fusion.2
  82.2 23.7 %all-gather.4.cloned.1.call-done = bf16[256,24,768]{2,1,0:T(8,128)(2,1)} async-done(((bf16[16,24,768]{2,1,0:T(8,128)(2,1)}), bf16[256,24,768]{2,1,0:T(8,128)(2,1)}) %all-gather.4.cloned.1.call-update) | async-done | bytes 9437200 | tf_op jit(solution)/shard_map/all_gather | solution.py:100
  105.9 12.8 %copy.64 = bf16[256,24,768]{0,2,1:T(8,128)(2,1)} copy(bf16[256,24,768]{2,1,0:T(8,128)(2,1)} %all-gather.4.cloned.1.call-done) | data formatting | bytes 18874368 | tf_op jit(solution)/shard_map/reshape | solution.py:105
  118.7 10.5 %fusion.26 = f32[2,2,24,2,384]{4,1,3,2,0:T(2,128)S(1)} fusion(bf16[24,2,384,256,1]{3,2,1,0,4:T(8,128)(2,1)} %bitcast.80, f32[2,2,256,1,1]{2,1,0,3,4:T(2,128)S(1)} %reshape.88), kind=kOutput, calls=%fused_computation.61 | convolution fusion | flops 226492416 | bytes 9736192 | tf_op jit(solution)/shard_map/dot_general | solution.py:107
  129.3 0.0 copy-done.1
  129.3 3.2 %fusion.41 = f32[2,64,24,2,384]{4,1,3,2,0:T(8,128)S(1)} fusion(bf16[2,64,256,1,1]{2,1,4,3,0:T(8,128)(2,1)S(1)} %bitcast.85, bf16[24,2,384,256,1]{3,2,1,0,4:T(8,128)(2,1)S(1)} %bitcast.81), kind=kOutput, calls=%fused_computation.80 | convolution fusion | flops 1207959552 | bytes 18939904 | tf_op jit(solution)/shard_map/dot_general | solution.py:104
  132.5 0.3 fusion.1
  132.9 0.3 fusion.3
  133.2 0.1 pad_maximum_fusion
  133.3 0.7 copy.61
  134.0 0.5 fusion
  134.5 2.7 %copy.60 = bf16[64,24,768]{2,1,0:T(8,128)(2,1)} copy(bf16[64,24,768]{2,0,1:T(8,128)(2,1)S(1)} %fusion) | data formatting | bytes 4718592
  (13 shorter events, 0.2 us)
Async XLA Ops:
  7.2 64.5 %copy-start = (s32[3,32]{1,0:T(4,128)S(1)}, s32[3,32]{1,0:T(4,128)}, u32[]{:S(2)}) copy-start(s32[3,32]{1,0:T(4,128)} %param.11) | copy-start | bytes 1156
  7.2 98.7 %all-gather.4.cloned.1.call-start = ((), (), s32[]{:S(2)}) async-start(), calls=%async_computation.1 | async-start | bytes 10027008 | tf_op jit(solution)/shard_map/all_gather | solution.py:100
  46.1 1.4 copy-start.2
  46.1 1.5 %copy-start.4 = (s32[64]{0:T(128)S(1)}, s32[64]{0:T(128)}, u32[]{:S(2)}) copy-start(s32[64]{0:T(128)} %param.10) | copy-start | bytes 772
  46.1 25.3 %copy-start.3 = (s32[3,256]{1,0:T(4,128)S(1)}, s32[3,256]{1,0:T(4,128)}, u32[]{:S(2)}) copy-start(s32[3,256]{1,0:T(4,128)} %param.8) | copy-start | bytes 9220
  118.7 10.6 %copy-start.1 = (bf16[256,24,768]{0,2,1:T(8,128)(2,1)S(1)}, bf16[256,24,768]{0,2,1:T(8,128)(2,1)}, u32[]{:S(2)}) copy-start(bf16[256,24,768]{0,2,1:T(8,128)(2,1)} %copy.64) | copy-start | bytes 28311556
Sparse Core Ops, SparseCore 0:
  47.7 58.2 all-gather.3
where the time goes:
time: 145 us; the launch traced here: 144 us
  blocking collectives  52.4 us (36%)
  waiting for transfers between devices  23.7 us (16%)
  matrix products  23.3 us (16%)
  local copies, waits for them, and re-layouts  21.1 us (15%)
  between operations  14.2 us (10%)
  other arithmetic  9.22 us (6%)
    all_to_all x1, blocking collectives, local(): lax.all_to_all(rotated, 'ka', split_axis=1, concat_axis=0, tiled=True)  29 us
    all_gather x1, waiting for transfers between devices, local(): k_piece = lax.all_gather(arrived, 'row', axis=0, tiled=True)  23.7 us
    all_gather x1, blocking collectives, gather_together(): lines, at, done = (lax.all_gather(vector, axis), 0, [])  23.4 us
    reshape x1, local copies, waits for them, and re-layouts, local(): k_piece.reshape(fourier_amount, -1)  12.8 us
    dot_general x1, matrix products, local(): jnp.dot(mixing, k_piece.reshape(amount, -1).astype(jnp.float32), preferre...  10.5 us
    unnamed x17, local copies, waits for them, and re-layouts  5.44 us
    unnamed x2, other arithmetic  5.07 us
    dot_general x1, matrix products, local(): jnp.dot(factors_path, factors_mesh[total_vectors:], preferred_element_typ...  4.48 us
  transfers between devices with their start and end apart: 1, of which 1 were waited for; matrix products, arithmetic and copies ran while one was open for 8% of the time, Pallas kernels for 0%

commit v1 on v0

v1 whole, which is shorter than its diff:
```python
import functools
import math

import jax
import jax.numpy as jnp
from jax import lax
from jax.experimental import pallas as pl
from jax.experimental.pallas import tpu as pltpu
from jax.sharding import PartitionSpec as P

MESH = 12
PATH_DEN = 64
NKA = 16
NROW = 16
ROWS = 24
TILES = 3
PARTS = 2
HALF = ROWS // 2
SUB = HALF // PARTS
CHUNKS = TILES * PARTS
UNIT = 2 * SUB
Y_FIRST = ()

BF = jnp.bfloat16
F32 = jnp.float32


def kernel(
    gauge, energies, kmesh, lattice, degeneracy, path,
    out_l, out_p,
    at_ref, sc_ref, send, arrived, plain, other, gath, lmat, fpart, mixp, mixr,
    stage_l, stage_p,
    a2a_s, a2a_r, g_s, g_r, f_s, f_r, m_s, m_r, o_s, o_r, op_s, op_r,
):
    ka = lax.axis_index("ka")
    row = lax.axis_index("row")
    core = row % 2
    y = (row // 2) % 4
    zlo = row // 8
    mate = row + 1 - 2 * core

    def unit_of(z, yy, c):
        return z * 8 + yy * 2 + c

    yp = (y + 1) % 4
    ym = (y + 3) % 4
    yo = (y + 2) % 4
    zo = 1 - zlo

    barrier = pltpu.get_barrier_semaphore()
    for i in range(1, NKA):
        pl.semaphore_signal(
            barrier, inc=1, device_id=((ka + i) % NKA, row), device_id_type=pl.DeviceIdType.MESH
        )
    for i in range(1, NROW):
        pl.semaphore_signal(
            barrier, inc=1, device_id=(ka, (row + i) % NROW), device_id_type=pl.DeviceIdType.MESH
        )

    def remote(src, dst, ssem, rsem, dev):
        return pltpu.make_async_remote_copy(
            src_ref=src, dst_ref=dst, send_sem=ssem, recv_sem=rsem,
            device_id=dev, device_id_type=pl.DeviceIdType.MESH,
        )

    def wait_bytes(ref, sem):
        pltpu.make_async_copy(ref, ref, sem).wait()

    w = gauge.shape[1]
    e_col = jnp.transpose(jnp.broadcast_to(energies[...], (128, w)))
    e_full = jnp.concatenate([e_col] * (w // 128), 1)
    for p in range(2):
        u = gauge[p].astype(F32)
        at_ref[:, p * w : (p + 1) * w] = jnp.transpose(u).astype(BF)
        sc_ref[p] = (e_full * u).astype(BF)

    def rotate(cc):
        cols = slice(cc * 128, cc * 128 + 128)
        sr = sc_ref[0, :, cols]
        si = sc_ref[1, :, cols]
        rhs = jnp.concatenate(
            [jnp.concatenate([sr, si], 1), jnp.concatenate([si, -sr], 1)], 0
        )
        h = jnp.dot(at_ref[...], rhs, preferred_element_type=F32)
        for j in range(NKA):
            both = jnp.concatenate(
                [h[j * ROWS : (j + 1) * ROWS, :128], h[j * ROWS : (j + 1) * ROWS, 128:]], 0
            )
            send[cc, j] = both.astype(BF)

    def spread(cc):
        for i in range(1, NKA):
            j = (ka + i) % NKA
            remote(send.at[cc, j], arrived.at[cc, ka], a2a_s.at[cc], a2a_r.at[cc], (j, row)).start()
        arrived[cc, pl.ds(ka, 1)] = send[cc, pl.ds(ka, 1)]

    rotate(0)
    pl.semaphore_wait(barrier, NKA - 1 + NROW - 1)
    spread(0)
    rotate(1)
    spread(1)
    rotate(2)

    nk = kmesh.shape[1]
    r_dev = lattice.shape[1]
    np_all = path.shape[1]

    def pad_rows(a):
        return jnp.concatenate([a.astype(F32), jnp.zeros((13, a.shape[1]), F32)], 0).astype(BF)

    lat = pad_rows(lattice[...])
    at_k = lax.broadcasted_iota(jnp.int32, (nk, nk), 0)
    to_k = lax.broadcasted_iota(jnp.int32, (nk, nk), 1)
    order = jnp.where(at_k == (to_k % NROW) * NROW + to_k // NKA, 1.0, 0.0).astype(BF)
    km = jnp.dot(pad_rows(kmesh[...]), order, preferred_element_type=F32).astype(BF)
    dims = (((0,), (0,)), ((), ()))
    wind = lax.dot_general(lat, km, dims, preferred_element_type=F32).astype(jnp.int32)
    wind = jnp.mod(wind + 23 * MESH, MESH)
    angle = wind.astype(F32) * (2.0 * math.pi / MESH)
    fcos = jnp.cos(angle).astype(BF)
    fsin = jnp.sin(angle).astype(BF)
    fpart[0, :, :nk] = fcos
    fpart[0, :, nk:] = fsin
    f_copy = remote(fpart.at[0], fpart.at[1], f_s, f_r, (ka, mate))
    f_copy.start()
    wind_p = lax.dot_general(pad_rows(path[...]), lat, dims, preferred_element_type=F32)
    wind_p = jnp.mod(wind_p.astype(jnp.int32) + 24 * PATH_DEN, PATH_DEN)
    angle_p = wind_p.astype(F32) * (2.0 * math.pi / PATH_DEN)
    weights = 1.0 / degeneracy[...].astype(F32)
    pcos = (jnp.cos(angle_p) * weights).astype(BF)
    psin = (jnp.sin(angle_p) * weights).astype(BF)
    pboth = jnp.concatenate([pcos, psin], 0)
    mc = jnp.dot(pboth, fcos, preferred_element_type=F32)
    ms = jnp.dot(pboth, fsin, preferred_element_type=F32)
    m_re = mc[:np_all] + ms[np_all:]
    m_im = mc[np_all:] - ms[:np_all]
    per_chip = np_all // (NROW // 2)
    for p in range(NROW // 2):
        mixp[p, :per_chip] = m_re[p * per_chip : (p + 1) * per_chip]
        mixp[p, per_chip:] = m_im[p * per_chip : (p + 1) * per_chip]
    for i in range(1, NROW):
        to = (row + i) % NROW
        remote(mixp.at[to // 2], mixr.at[row], m_s, m_r, (ka, to)).start()
    mixr[pl.ds(row, 1)] = mixp[pl.ds(row // 2, 1)]

    def transpose(cc):
        wait_bytes(arrived.at[cc, pl.ds(0, NKA - 1)], a2a_r.at[cc])
        plain[...] = arrived[cc].reshape(NKA * 2 * ROWS, 128).astype(F32)
        for part in range(PARTS):
            g = cc * PARTS + part
            for p in range(2):
                for a in range(SUB):
                    at = p * ROWS + part * SUB + a
                    mine = plain[pl.ds(at + core * HALF, NKA, stride=2 * ROWS), :]
                    gath[g, row, p * SUB + a] = mine.astype(BF)
                    his = plain[pl.ds(at + (1 - core) * HALF, NKA, stride=2 * ROWS), :]
                    other[g, p * SUB + a] = his.astype(BF)
            remote(other.at[g], gath.at[g, row], g_s.at[g], g_r.at[g, row], (ka, mate)).start()
            scatter(g, row)

    def pass_on(g, u, to):
        remote(gath.at[g, u], gath.at[g, u], g_s.at[g], g_r.at[g, u], (ka, to)).start()

    def landed(g, u):
        wait_bytes(gath.at[g, u], g_r.at[g, u])

    def scatter(g, u):
        pass_on(g, u, unit_of(zlo, yp, core))
        pass_on(g, u, unit_of(zlo, ym, core))
        if g not in Y_FIRST:
            pass_on(g, u, unit_of(zo, y, core))

    def from_mate(g):
        landed(g, mate)
        scatter(g, mate)

    def relay(g, z):
        for c in range(2):
            um = unit_of(z, ym, c)
            landed(g, um)
            if c == 0:
                pass_on(g, um, unit_of(zlo, yp, core))
            if g in Y_FIRST:
                pass_on(g, um, unit_of(zo, y, core))
            up = unit_of(z, yp, c)
            landed(g, up)
            if c == 1:
                pass_on(g, up, unit_of(zlo, ym, core))
            if g in Y_FIRST:
                pass_on(g, up, unit_of(zo, y, core))

    def y_far(g, z):
        for c in range(2):
            u = unit_of(z, yo, c)
            landed(g, u)
            if g in Y_FIRST:
                pass_on(g, u, unit_of(zo, y, core))

    def own_plane(g):
        relay(g, zlo)
        if g in Y_FIRST:
            for c in range(2):
                u = unit_of(zlo, y, c)
                pass_on(g, u, unit_of(zo, y, core))
            y_far(g, zlo)

    def z_arrivals(g):
        if g in Y_FIRST:
            return
        for c in range(2):
            u = unit_of(zo, y, c)
            landed(g, u)
            pass_on(g, u, unit_of(zlo, yp, core))
            pass_on(g, u, unit_of(zlo, ym, core))

    def other_plane(g):
        if g not in Y_FIRST:
            relay(g, zo)

    def last_units(g):
        if g in Y_FIRST:
            for yy in range(4):
                for c in range(2):
                    landed(g, unit_of(zo, yy, c))
        else:
            y_far(g, zlo)
            y_far(g, zo)

    def build_factors():
        wait_bytes(mixr.at[pl.ds(0, NROW - 1)], m_r)
        f_copy.wait()
        for s in range(2):
            at = s * 2 * r_dev
            c_part = fpart[s, :, :nk]
            s_part = fpart[s, :, nk:]
            lmat[at : at + r_dev, :nk] = c_part
            lmat[at : at + r_dev, nk:] = s_part
            lmat[at + r_dev : at + 2 * r_dev, :nk] = -s_part
            lmat[at + r_dev : at + 2 * r_dev, nk:] = c_part
        total = mixr[0]
        for i in range(1, NROW):
            total = total + mixr[i]
        m_r4 = total[:per_chip]
        m_i4 = total[per_chip:]
        wide = jnp.concatenate(
            [jnp.concatenate([m_r4, -m_i4], 1), jnp.concatenate([m_i4, m_r4], 1)], 0
        )
        high = wide.astype(BF)
        low = (wide - high.astype(F32)).astype(BF)
        lmat[4 * r_dev :, :] = jnp.concatenate([high.astype(F32), low.astype(F32)], 0).astype(BF)

    scale = 1.0 / nk

    def transform(g):
        last_units(g)

        def one(i, carry):
            a = 2 * i
            re0 = gath[g, :, a].reshape(nk, 128)
            re1 = gath[g, :, a + 1].reshape(nk, 128)
            im0 = gath[g, :, SUB + a].reshape(nk, 128)
            im1 = gath[g, :, SUB + a + 1].reshape(nk, 128)
            x = jnp.concatenate(
                [jnp.concatenate([re0, re1], 1), jnp.concatenate([im0, im1], 1)], 0
            )
            y_all = jnp.dot(lmat[...], x, preferred_element_type=F32) * scale
            for b in range(2):
                v = y_all[:, b * 128 : b * 128 + 128]
                for p in range(2):
                    out_l[core, g, p, a + b] = v[p * r_dev : (p + 1) * r_dev].astype(BF)
                    stage_l[g, p, a + b] = v[(2 + p) * r_dev : (3 + p) * r_dev].astype(BF)
                vp = v[4 * r_dev : 4 * r_dev + 8] + v[4 * r_dev + 8 :]
                out_p[core, g, a + b] = vp
                stage_p[g, a + b] = vp
            return carry

        lax.fori_loop(0, SUB // 2, one, 0)
        remote(stage_l.at[g], out_l.at[core, g], o_s.at[g], o_r.at[g], (ka, mate)).start()
        remote(stage_p.at[g], out_p.at[core, g], op_s.at[g], op_r.at[g], (ka, mate)).start()

    transpose(0)
    from_mate(0)
    from_mate(1)
    spread(2)
    own_plane(0)
    own_plane(1)
    transpose(1)
    from_mate(2)
    from_mate(3)
    z_arrivals(0)
    z_arrivals(1)
    other_plane(0)
    other_plane(1)
    transpose(2)
    from_mate(4)
    from_mate(5)
    own_plane(2)
    own_plane(3)
    build_factors()
    z_arrivals(2)
    z_arrivals(3)
    transform(0)
    transform(1)
    other_plane(2)
    other_plane(3)
    own_plane(4)
    own_plane(5)
    z_arrivals(4)
    z_arrivals(5)
    transform(2)
    transform(3)
    other_plane(4)
    other_plane(5)
    transform(4)
    transform(5)

    for cc in range(TILES):
        wait_bytes(send.at[cc, pl.ds(0, NKA - 1)], a2a_s.at[cc])
    wait_bytes(mixr.at[pl.ds(0, NROW - 1)], m_s)
    for g in range(CHUNKS):
        wait_bytes(gath.at[g, pl.ds(0, NROW - 1)], g_s.at[g])
        wait_bytes(stage_l.at[g], o_s.at[g])
        wait_bytes(stage_p.at[g], op_s.at[g])
        wait_bytes(stage_l.at[g], o_r.at[g])
        wait_bytes(stage_p.at[g], op_r.at[g])


def local(gauge, energies, kmesh, lattice, degeneracy, path):
    w = gauge.shape[2]
    nk = kmesh.shape[1]
    r_dev = lattice.shape[1]
    path_dev = path.shape[1] // NROW
    vmem = pl.BlockSpec(memory_space=pltpu.VMEM)
    dma = pltpu.SemaphoreType.DMA
    out_l, out_p = pl.pallas_call(
        kernel,
        out_shape=(
            jax.ShapeDtypeStruct((2, CHUNKS, 2, SUB, r_dev, 128), BF),
            jax.ShapeDtypeStruct((2, CHUNKS, SUB, 8, 128), F32),
        ),
        in_specs=[vmem] * 6,
        out_specs=(vmem, vmem),
        scratch_shapes=[
            pltpu.VMEM((w, 2 * w), BF),
            pltpu.VMEM((2, w, w), BF),
            pltpu.VMEM((TILES, NKA, 2 * ROWS, 128), BF),
            pltpu.VMEM((TILES, NKA, 2 * ROWS, 128), BF),
            pltpu.VMEM((NKA * 2 * ROWS, 128), F32),
            pltpu.VMEM((CHUNKS, UNIT, NKA, 128), BF),
            pltpu.VMEM((CHUNKS, NROW, UNIT, NKA, 128), BF),
            pltpu.VMEM((4 * r_dev + 16, 2 * nk), BF),
            pltpu.VMEM((2, r_dev, 2 * nk), BF),
            pltpu.VMEM((NROW // 2, 8, nk), F32),
            pltpu.VMEM((NROW, 8, nk), F32),
            pltpu.VMEM((CHUNKS, 2, SUB, r_dev, 128), BF),
            pltpu.VMEM((CHUNKS, SUB, 8, 128), F32),
            dma((TILES,)),
            dma((TILES,)),
            dma((CHUNKS,)),
            dma((CHUNKS, NROW)),
            dma,
            dma,
            dma,
            dma,
            dma((CHUNKS,)),
            dma((CHUNKS,)),
            dma((CHUNKS,)),
            dma((CHUNKS,)),
        ],
        compiler_params=pltpu.CompilerParams(
            collective_id=0, has_side_effects=True, vmem_limit_bytes=40 << 20
        ),
    )(gauge[0], energies, kmesh, lattice, degeneracy[None, :], path)
    lat = out_l.reshape(2, TILES, PARTS, 2, SUB, r_dev, 128)
    lattice_h = lat.transpose(5, 0, 2, 4, 3, 1, 6).reshape(r_dev, ROWS, 2 * w)
    core = lax.axis_index("row") % 2
    pth = out_p.reshape(2, TILES, PARTS, SUB, 2, 2, path_dev, 128)
    pth = lax.dynamic_index_in_dim(pth, core, 5, keepdims=False)
    path_h = pth.transpose(5, 0, 2, 3, 4, 1, 6).reshape(path_dev, ROWS, 2 * w)
    return lattice_h, path_h


def solution(mesh):
    return jax.shard_map(
        local,
        mesh=mesh,
        in_specs=(
            P(("ka", "row"), None, None, None),
            P(("ka", "row"), None),
            P(),
            P(None, "row"),
            P("row"),
            P(),
        ),
        out_specs=(P("row", "ka", None), P("row", "ka", None)),
        check_vma=False,
    )
```

time: 145 us -> 83.8 us (0.58)
  Pallas kernels: 0 us -> 67 us
  blocking collectives: 52.4 us -> 0 us
  waiting for transfers between devices: 23.7 us -> 0 us
  matrix products: 23.3 us -> 0 us
  between operations: 14.2 us -> 0.68 us
  other arithmetic: 9.22 us -> 0 us
  local copies, waits for them, and re-layouts: 21.1 us -> 15.7 us
    pallas_call x0 -> x1, Pallas kernels: none -> 67 us  [local(): pl.pallas_call(kernel, out_shape=(jax.ShapeDtypeStruct((2, CHUNKS, 2, SUB...]
    all_to_all x1 -> x0, blocking collectives: 29 us -> none  [local(): lax.all_to_all(rotated, 'ka', split_axis=1, concat_axis=0, tiled=True)]
    all_gather x1 -> x0, waiting for transfers between devices: 23.7 us -> none  [local(): k_piece = lax.all_gather(arrived, 'row', axis=0, tiled=True)]
    all_gather x1 -> x0, blocking collectives: 23.4 us -> none  [gather_together(): lines, at, done = (lax.all_gather(vector, axis), 0, [])]
    dot_general x5 -> x0, matrix products: 23.3 us -> none  [the longest x1 10.5 us: local(): jnp.dot(mixing, k_piece.reshape(amount, -1).astype(jnp.float32), preferre...]
    unnamed x2 -> x0, other arithmetic: 5.07 us -> none
    reshape x5 -> x3, local copies, waits for them, and re-layouts: 13.1 us -> 11.2 us  [the longest x1 6.75 us: local(): lattice_h = lat.transpose(5, 0, 2, 4, 3, 1, 6).reshape(r_dev, ROWS, 2 * w)]
    convert_element_type x2 -> x0, other arithmetic: 1.75 us -> none  [the longest x1 1.23 us: local(): (energies[:, None, :, None] * gauge.astype(jnp.float32)).astype(jnp.bfloa...]
  transfers between devices with their start and end apart: 1 -> 0, of which waited for: 1 -> 0; matrix products, arithmetic and copies ran while one was open for 8% -> 0% of each run, Pallas kernels for 0% -> 0%
where the time goes in v1:
time: 83.8 us; the launch traced here: 83.4 us
  Pallas kernels  67 us (80%)
  local copies, waits for them, and re-layouts  15.7 us (19%)
    pallas_call x1, Pallas kernels, local(): pl.pallas_call(kernel, out_shape=(jax.ShapeDtypeStruct((2, CHUNKS, 2, SUB...  67 us
    reshape x1, local copies, waits for them, and re-layouts, local(): lattice_h = lat.transpose(5, 0, 2, 4, 3, 1, 6).reshape(r_dev, ROWS, 2 * w)  6.75 us
    unnamed x12, local copies, waits for them, and re-layouts  4.44 us
    reshape x1, local copies, waits for them, and re-layouts, local(): lat = out_l.reshape(2, TILES, PARTS, 2, SUB, r_dev, 128)  3.67 us

profile of v1, /device:TPU:1, one launch (start us, length us, event | category | flops | bytes accessed | tf_op | source)
XLA Modules:
  0.0 83.4 jit_solution(15972954991550424518)
XLA Ops:
  0.6 0.0 copy-start
  0.7 1.1 %copy-done = bf16[1,2,384,384]{3,2,1,0:T(8,128)(2,1)S(1)} copy-done((bf16[1,2,384,384]{3,2,1,0:T(8,128)(2,1)S(1)}, bf16[1,2,384,384]{3,2,1,0:T(8,128)(2,1)}, u32[]{:S(2)}) %copy-start) | copy-done | bytes 589848
  1.7 0.0 copy-start.1
  1.7 0.7 copy-done.1
  2.4 0.0 copy-start.2
  2.4 0.7 copy-done.2
  3.1 0.0 copy-start.3
  3.1 0.7 copy-done.3
  3.8 0.0 copy-start.4
  3.8 0.7 copy-done.4
  4.4 0.0 copy-start.5
  4.4 0.7 copy-done.5
  5.1 67.0 %shard_map.77 = (bf16[2,6,2,6,64,128]{5,4,3,2,1,0:T(8,128)(2,1)S(1)}, f32[2,6,6,8,128]{4,3,2,1,0:T(8,128)S(1)}) custom-call(bf16[2,384,384]{2,1,0:T(8,128)(2,1)S(1)} %bitcast.14, f32[1,384]{1,0:T(1,128)S(1)} %copy-done.4, s32[3,256]{1,0:T(4,128)S(1)} %copy-done.1, s32[3,64]{1,0:T(4,128)S(1)} %copy-done.2, s32[1,64]{1,0:T(1,128)S(1)} %bitcast.16, ...), custom_call_target="tpu_custom_call" | custom-call | tf_op jit(solution)/shard_map/pallas_call | solution.py:335
  72.1 0.1 dynamic-slice_bitcast_fusion
  72.1 0.1 copy.11
  72.2 0.7 reshape.19
  73.0 3.7 %copy.14 = bf16[2,3,2,2,6,64,128]{6,1,3,4,2,0,5:T(4,128)(2,1)} copy(bf16[2,3,2,2,6,64,128]{6,5,4,3,2,1,0:T(8,128)(2,1)S(1)} %bitcast.13) | data formatting | bytes 4718592 | tf_op jit(solution)/shard_map/reshape | solution.py:374
  76.6 6.7 %reshape.17 = bf16[64,24,768]{2,1,0:T(8,128)(2,1)} reshape(bf16[64,2,2,6,2,3,128]{6,5,4,3,2,1,0:T(4,128)(2,1)} %bitcast.17) | data formatting | bytes 4718592 | tf_op jit(solution)/shard_map/reshape | solution.py:375
Async XLA Ops:
  0.6 1.1 %copy-start = (bf16[1,2,384,384]{3,2,1,0:T(8,128)(2,1)S(1)}, bf16[1,2,384,384]{3,2,1,0:T(8,128)(2,1)}, u32[]{:S(2)}) copy-start(bf16[1,2,384,384]{3,2,1,0:T(8,128)(2,1)} %param.6) | copy-start | bytes 1769476
  1.7 0.7 copy-start.1
  2.4 0.7 copy-start.2
  3.1 0.7 copy-start.3
  3.8 0.7 copy-start.4
  4.4 0.7 copy-start.5

commit v2 on v1

--- a/solution.py
+++ b/solution.py
@@ -19,24 +19,44 @@
 SUB = HALF // PARTS
 CHUNKS = TILES * PARTS
 UNIT = 2 * SUB
-Y_FIRST = ()
+Y_FIRST = (3,)
 
 BF = jnp.bfloat16
 F32 = jnp.float32
 
 
 def kernel(
-    gauge, energies, kmesh, lattice, degeneracy, path,
+    gauge_h, energies_h, kmesh_h, lattice_h, degeneracy_h, path_h,
     out_l, out_p,
+    gauge, energies, kmesh, lattice, degeneracy, path, in_s,
     at_ref, sc_ref, send, arrived, plain, other, gath, lmat, fpart, mixp, mixr,
-    stage_l, stage_p,
+    stage_l, stage_p, from_l, from_p, rows_f, rows_p, mix_f,
     a2a_s, a2a_r, g_s, g_r, f_s, f_r, m_s, m_r, o_s, o_r, op_s, op_r,
 ):
+    loads = [
+        pltpu.make_async_copy(src, dst, in_s.at[i])
+        for i, (src, dst) in enumerate(
+            (
+                (energies_h, energies), (gauge_h, gauge), (kmesh_h, kmesh),
+                (lattice_h, lattice), (degeneracy_h, degeneracy), (path_h, path),
+            )
+        )
+    ]
+    for load in loads:
+        load.start()
+
     ka = lax.axis_index("ka")
     row = lax.axis_index("row")
     core = row % 2
     y = (row // 2) % 4
     zlo = row // 8
+    x = ka // 4
+    z = (ka % 4) * 2 + zlo
+    turn = 2 * zlo - 1
+    peers = [(dx, d) for d in (3, 2, 1, 0) for dx in (2, 1, 3, 0) if dx or d]
+
+    def place_of(xx, zz):
+        return (xx % 4) * 4 + zz // 2, (zz % 2) * 8 + row % 8
     mate = row + 1 - 2 * core
 
     def unit_of(z, yy, c):
@@ -48,9 +68,10 @@
     zo = 1 - zlo
 
     barrier = pltpu.get_barrier_semaphore()
-    for i in range(1, NKA):
+    for dx, d in peers:
         pl.semaphore_signal(
-            barrier, inc=1, device_id=((ka + i) % NKA, row), device_id_type=pl.DeviceIdType.MESH
+            barrier, inc=1, device_id=place_of(x + dx, (z + turn * d + 8) % 8),
+            device_id_type=pl.DeviceIdType.MESH,
         )
     for i in range(1, NROW):
         pl.semaphore_signal(
@@ -66,6 +87,8 @@
     def wait_bytes(ref, sem):
         pltpu.make_async_copy(ref, ref, sem).wait()
 
+    loads[0].wait()
+    loads[1].wait()
     w = gauge.shape[1]
     e_col = jnp.transpose(jnp.broadcast_to(energies[...], (128, w)))
     e_full = jnp.concatenate([e_col] * (w // 128), 1)
@@ -89,10 +112,12 @@
             send[cc, j] = both.astype(BF)
 
     def spread(cc):
-        for i in range(1, NKA):
-            j = (ka + i) % NKA
-            remote(send.at[cc, j], arrived.at[cc, ka], a2a_s.at[cc], a2a_r.at[cc], (j, row)).start()
-        arrived[cc, pl.ds(ka, 1)] = send[cc, pl.ds(ka, 1)]
+        for dx, d in peers:
+            to = place_of(x + dx, (z + turn * (0, 1, -2, 3)[d] + 8) % 8)
+            remote(
+                send.at[cc, to[0]], arrived.at[cc, x * 4 + d], a2a_s.at[cc], a2a_r.at[cc], to
+            ).start()
+        arrived[cc, pl.ds(x * 4, 1)] = send[cc, pl.ds(ka, 1)]
 
     rotate(0)
     pl.semaphore_wait(barrier, NKA - 1 + NROW - 1)
@@ -101,6 +126,8 @@
     spread(1)
     rotate(2)
 
+    for load in loads[2:]:
+        load.wait()
     nk = kmesh.shape[1]
     r_dev = lattice.shape[1]
     np_all = path.shape[1]
@@ -110,8 +137,11 @@
 
     lat = pad_rows(lattice[...])
     at_k = lax.broadcasted_iota(jnp.int32, (nk, nk), 0)
-    to_k = lax.broadcasted_iota(jnp.int32, (nk, nk), 1)
-    order = jnp.where(at_k == (to_k % NROW) * NROW + to_k // NKA, 1.0, 0.0).astype(BF)
+    pos = lax.broadcasted_iota(jnp.int32, (8, nk), 1)
+    pos_z = pos >> 7
+    from_z = ((ka % 4) * 2 + pos_z + (2 * pos_z - 1) * (pos & 3) + 8) & 7
+    source = ((((pos >> 2) & 3) * 4 + (from_z >> 1)) * NROW) + (from_z & 1) * 8 + ((pos >> 4) & 7)
+    order = jnp.where(at_k == source[:1], 1.0, 0.0).astype(BF)
     km = jnp.dot(pad_rows(kmesh[...]), order, preferred_element_type=F32).astype(BF)
     dims = (((0,), (0,)), ((), ()))
     wind = lax.dot_general(lat, km, dims, preferred_element_type=F32).astype(jnp.int32)
@@ -245,6 +275,10 @@
         wide = jnp.concatenate(
             [jnp.concatenate([m_r4, -m_i4], 1), jnp.concatenate([m_i4, m_r4], 1)], 0
         )
+        own_q = per_chip // 2
+        for i in range(4):
+            mix_f[i] = wide[i * own_q : (i + 1) * own_q]
+        wide = jnp.concatenate([mix_f[2 * p + c] for c in (core, 1 - core) for p in range(2)], 0)
         high = wide.astype(BF)
         low = (wide - high.astype(F32)).astype(BF)
         lmat[4 * r_dev :, :] = jnp.concatenate([high.astype(F32), low.astype(F32)], 0).astype(BF)
@@ -253,6 +287,8 @@
 
     def transform(g):
         last_units(g)
+        cc = g // PARTS
+        first = (g % PARTS) * SUB
 
         def one(i, carry):
             a = 2 * i
@@ -267,16 +303,54 @@
             for b in range(2):
                 v = y_all[:, b * 128 : b * 128 + 128]
                 for p in range(2):
-                    out_l[core, g, p, a + b] = v[p * r_dev : (p + 1) * r_dev].astype(BF)
+                    place(cc, p, core * HALF + first + a + b, v[p * r_dev : (p + 1) * r_dev])
                     stage_l[g, p, a + b] = v[(2 + p) * r_dev : (3 + p) * r_dev].astype(BF)
                 vp = v[4 * r_dev : 4 * r_dev + 8] + v[4 * r_dev + 8 :]
-                out_p[core, g, a + b] = vp
+                place_path(cc, core * HALF + first + a + b, vp[:4])
                 stage_p[g, a + b] = vp
             return carry
 
         lax.fori_loop(0, SUB // 2, one, 0)
-        remote(stage_l.at[g], out_l.at[core, g], o_s.at[g], o_r.at[g], (ka, mate)).start()
-        remote(stage_p.at[g], out_p.at[core, g], op_s.at[g], op_r.at[g], (ka, mate)).start()
+        remote(stage_l.at[g], from_l.at[g], o_s.at[g], o_r.at[g], (ka, mate)).start()
+        remote(stage_p.at[g], from_p.at[g], op_s.at[g], op_r.at[g], (ka, mate)).start()
+
+    def place(cc, p, a, value):
+        rows_f[cc, p, pl.ds(a, r_dev, stride=ROWS), :] = value
+
+    def place_path(cc, a, value):
+        for p in range(2):
+            rows_p[cc, p, pl.ds(a, 2, stride=ROWS), :] = value[2 * p : 2 * p + 2]
+
+    def from_other_core(g):
+        cc = g // PARTS
+        first = (1 - core) * HALF + (g % PARTS) * SUB
+        wait_bytes(stage_l.at[g], o_r.at[g])
+        wait_bytes(stage_p.at[g], op_r.at[g])
+
+        def one(a, carry):
+            for p in range(2):
+                place(cc, p, first + a, from_l[g, p, a].astype(F32))
+            place_path(cc, first + a, from_p[g, a, 4:])
+            return carry
+
+        lax.fori_loop(0, SUB, one, 0)
+
+    def write_out(cc):
+        step = 8
+
+        def one(i, carry):
+            at = pl.multiple_of(i * step * ROWS, step * ROWS)
+            for p in range(2):
+                cols = slice((p * TILES + cc) * 128, (p * TILES + cc + 1) * 128)
+                block = rows_f[cc, p, pl.ds(at, step * ROWS), :].astype(BF)
+                out_l[pl.ds(i * step, step), :, cols] = block.reshape(step, ROWS, 128)
+            return carry
+
+        lax.fori_loop(0, r_dev // step, one, 0)
+        for p in range(2):
+            cols = slice((p * TILES + cc) * 128, (p * TILES + cc + 1) * 128)
+            for q in range(2):
+                out_p[q, :, cols] = rows_p[cc, p, q * ROWS : (q + 1) * ROWS, :]
 
     transpose(0)
     from_mate(0)
@@ -309,10 +383,19 @@
     z_arrivals(5)
     transform(2)
     transform(3)
+    from_other_core(0)
+    from_other_core(1)
+    write_out(0)
     other_plane(4)
     other_plane(5)
+    from_other_core(2)
+    from_other_core(3)
+    write_out(1)
     transform(4)
     transform(5)
+    from_other_core(4)
+    from_other_core(5)
+    write_out(2)
 
     for cc in range(TILES):
         wait_bytes(send.at[cc, pl.ds(0, NKA - 1)], a2a_s.at[cc])
@@ -321,8 +404,6 @@
         wait_bytes(gath.at[g, pl.ds(0, NROW - 1)], g_s.at[g])
         wait_bytes(stage_l.at[g], o_s.at[g])
         wait_bytes(stage_p.at[g], op_s.at[g])
-        wait_bytes(stage_l.at[g], o_r.at[g])
-        wait_bytes(stage_p.at[g], op_r.at[g])
 
 
 def local(gauge, energies, kmesh, lattice, degeneracy, path):
@@ -332,15 +413,23 @@
     path_dev = path.shape[1] // NROW
     vmem = pl.BlockSpec(memory_space=pltpu.VMEM)
     dma = pltpu.SemaphoreType.DMA
-    out_l, out_p = pl.pallas_call(
+    hbm = pl.BlockSpec(memory_space=pltpu.HBM)
+    return pl.pallas_call(
         kernel,
         out_shape=(
-            jax.ShapeDtypeStruct((2, CHUNKS, 2, SUB, r_dev, 128), BF),
-            jax.ShapeDtypeStruct((2, CHUNKS, SUB, 8, 128), F32),
+            jax.ShapeDtypeStruct((r_dev, ROWS, 2 * w), BF),
+            jax.ShapeDtypeStruct((path_dev, ROWS, 2 * w), F32),
         ),
-        in_specs=[vmem] * 6,
+        in_specs=[hbm] * 6,
         out_specs=(vmem, vmem),
         scratch_shapes=[
+            pltpu.VMEM((2, w, w), BF),
+            pltpu.VMEM((1, w), F32),
+            pltpu.VMEM((3, nk), jnp.int32),
+            pltpu.VMEM((3, r_dev), jnp.int32),
+            pltpu.VMEM((1, r_dev), jnp.int32),
+            pltpu.VMEM(path.shape, jnp.int32),
+            dma((6,)),
             pltpu.VMEM((w, 2 * w), BF),
             pltpu.VMEM((2, w, w), BF),
             pltpu.VMEM((TILES, NKA, 2 * ROWS, 128), BF),
@@ -354,6 +443,11 @@
             pltpu.VMEM((NROW, 8, nk), F32),
             pltpu.VMEM((CHUNKS, 2, SUB, r_dev, 128), BF),
             pltpu.VMEM((CHUNKS, SUB, 8, 128), F32),
+            pltpu.VMEM((CHUNKS, 2, SUB, r_dev, 128), BF),
+            pltpu.VMEM((CHUNKS, SUB, 8, 128), F32),
+            pltpu.VMEM((TILES, 2, r_dev * ROWS, 128), F32),
+            pltpu.VMEM((TILES, 2, path_dev * ROWS, 128), F32),
+            pltpu.VMEM((4, path_dev, 2 * nk), F32),
             dma((TILES,)),
             dma((TILES,)),
             dma((CHUNKS,)),
@@ -368,16 +462,9 @@
             dma((CHUNKS,)),
         ],
         compiler_params=pltpu.CompilerParams(
-            collective_id=0, has_side_effects=True, vmem_limit_bytes=40 << 20
+            collective_id=0, has_side_effects=True, vmem_limit_bytes=48 << 20
         ),
-    )(gauge[0], energies, kmesh, lattice, degeneracy[None, :], path)
-    lat = out_l.reshape(2, TILES, PARTS, 2, SUB, r_dev, 128)
-    lattice_h = lat.transpose(5, 0, 2, 4, 3, 1, 6).reshape(r_dev, ROWS, 2 * w)
-    core = lax.axis_index("row") % 2
-    pth = out_p.reshape(2, TILES, PARTS, SUB, 2, 2, path_dev, 128)
-    pth = lax.dynamic_index_in_dim(pth, core, 5, keepdims=False)
-    path_h = pth.transpose(5, 0, 2, 3, 4, 1, 6).reshape(path_dev, ROWS, 2 * w)
-    return lattice_h, path_h
+    )(*[pltpu.with_memory_space_constraint(v, pltpu.HBM) for v in (gauge[0], energies, kmesh, lattice, degeneracy[None, :], path)])
 
 
 def solution(mesh):

time: 83.8 us -> 68.2 us (0.81)
  local copies, waits for them, and re-layouts: 15.7 us -> 2.07 us
  Pallas kernels: 67 us -> 65.3 us
    reshape x3 -> x0, local copies, waits for them, and re-layouts: 11.2 us -> none  [the longest x1 6.75 us: local(): lattice_h = lat.transpose(5, 0, 2, 4, 3, 1, 6).reshape(r_dev, ROWS, 2 * w)]
    unnamed x12 -> x2, local copies, waits for them, and re-layouts: 4.44 us -> 2.07 us
    pallas_call x1, Pallas kernels: 67 us -> 65.3 us  [local(): pl.pallas_call(kernel, out_shape=(jax.ShapeDtypeStruct((r_dev, ROWS, 2 *...]
where the time goes in v2:
time: 68.2 us; the launch traced here: 68 us
  Pallas kernels  65.3 us (96%)
  local copies, waits for them, and re-layouts  2.07 us (3%)
    pallas_call x1, Pallas kernels, local(): pl.pallas_call(kernel, out_shape=(jax.ShapeDtypeStruct((r_dev, ROWS, 2 *...  65.3 us
    unnamed x2, local copies, waits for them, and re-layouts  2.07 us

profile of v2, /device:TPU:1, one launch (start us, length us, event | category | flops | bytes accessed | tf_op | source)
XLA Modules:
  0.0 68.0 jit_solution(15785864198444139569)
XLA Ops:
  0.6 65.3 %shard_map.77 = (bf16[64,24,768]{2,1,0:T(8,128)(2,1)S(1)}, f32[2,24,768]{2,1,0:T(8,128)S(1)}) custom-call(bf16[2,384,384]{2,1,0:T(8,128)(2,1)} %bitcast.2, f32[1,384]{1,0:T(1,128)} %energies_h.1, s32[3,256]{1,0:T(4,128)} %kmesh_h.1, s32[3,64]{1,0:T(4,128)} %lattice_h.1, s32[1,64]{1,0:T(1,128)} %bitcast.3, s32[3,32]{1,0:T(4,128)} %path_h.1), custom_call_target="tpu_custom_call" | custom-call | tf_op jit(solution)/shard_map/pallas_call | solution.py:417
  65.9 1.4 %copy.10 = bf16[64,24,768]{2,1,0:T(8,128)(2,1)} copy(bf16[64,24,768]{2,1,0:T(8,128)(2,1)S(1)} %get-tuple-element.4) | data formatting | bytes 4718592
  67.3 0.7 copy.11

commit v3 on v2

--- a/solution.py
+++ b/solution.py
@@ -14,12 +14,19 @@
 NROW = 16
 ROWS = 24
 TILES = 3
-PARTS = 2
 HALF = ROWS // 2
-SUB = HALF // PARTS
-CHUNKS = TILES * PARTS
-UNIT = 2 * SUB
-Y_FIRST = (3,)
+PIECES = ((0, 0, 12), (1, 0, 6), (1, 6, 6), (2, 0, 4), (2, 4, 4), (2, 8, 4))
+Y_FIRST = (1, 2, 3,)
+ORDER = (
+    (0,0), (1,0,0,0,1), (0,1), (1,0,0,-1,0), (1,0,1,0,0), (1,1,0,0,1), (1,2,0,0,1), (1,0,0,1,1),
+    (1,0,1,0,1), (1,1,0,-1,0), (1,1,0,1,0), (0,2), (1,2,0,-1,0), (1,2,0,1,0), (1,3,0,0,1),
+    (1,4,0,0,1), (1,5,0,0,1), (1,1,0,1,1), (1,0,1,-1,0), (1,2,0,1,1), (1,1,0,-1,1), (1,4,1,0,0),
+    (1,5,1,0,0), (1,2,0,-1,1), (1,0,1,1,1), (1,3,0,1,0), (1,1,0,2,0), (1,4,1,0,1), (1,3,0,-1,0),
+    (1,5,1,0,1), (1,4,0,-1,0), (1,3,0,1,1), (1,5,0,-1,0), (1,4,0,1,1), (1,2,0,2,0), (1,5,0,1,1),
+    (1,3,0,-1,1), (1,1,0,2,1), (1,2,0,2,1), (1,4,1,-1,0), (1,5,1,-1,0), (2,0), (1,4,1,1,1),
+    (1,3,0,2,0), (1,5,1,1,1), (1,3,0,2,1), (2,1), (2,2), (2,4), (2,5), (2,3),
+)
+CHUNKS = len(PIECES)
 
 BF = jnp.bfloat16
 F32 = jnp.float32
@@ -125,6 +132,7 @@
     rotate(1)
     spread(1)
     rotate(2)
+    spread(2)
 
     for load in loads[2:]:
         load.wait()
@@ -173,88 +181,44 @@
         remote(mixp.at[to // 2], mixr.at[row], m_s, m_r, (ka, to)).start()
     mixr[pl.ds(row, 1)] = mixp[pl.ds(row // 2, 1)]
 
-    def transpose(cc):
+    def take_tile(cc):
         wait_bytes(arrived.at[cc, pl.ds(0, NKA - 1)], a2a_r.at[cc])
         plain[...] = arrived[cc].reshape(NKA * 2 * ROWS, 128).astype(F32)
-        for part in range(PARTS):
-            g = cc * PARTS + part
-            for p in range(2):
-                for a in range(SUB):
-                    at = p * ROWS + part * SUB + a
-                    mine = plain[pl.ds(at + core * HALF, NKA, stride=2 * ROWS), :]
-                    gath[g, row, p * SUB + a] = mine.astype(BF)
-                    his = plain[pl.ds(at + (1 - core) * HALF, NKA, stride=2 * ROWS), :]
-                    other[g, p * SUB + a] = his.astype(BF)
-            remote(other.at[g], gath.at[g, row], g_s.at[g], g_r.at[g, row], (ka, mate)).start()
-            scatter(g, row)
-
-    def pass_on(g, u, to):
-        remote(gath.at[g, u], gath.at[g, u], g_s.at[g], g_r.at[g, u], (ka, to)).start()
-
-    def landed(g, u):
-        wait_bytes(gath.at[g, u], g_r.at[g, u])
-
-    def scatter(g, u):
-        pass_on(g, u, unit_of(zlo, yp, core))
-        pass_on(g, u, unit_of(zlo, ym, core))
-        if g not in Y_FIRST:
-            pass_on(g, u, unit_of(zo, y, core))
-
-    def from_mate(g):
-        landed(g, mate)
-        scatter(g, mate)
-
-    def relay(g, z):
-        for c in range(2):
-            um = unit_of(z, ym, c)
-            landed(g, um)
-            if c == 0:
-                pass_on(g, um, unit_of(zlo, yp, core))
-            if g in Y_FIRST:
-                pass_on(g, um, unit_of(zo, y, core))
-            up = unit_of(z, yp, c)
-            landed(g, up)
-            if c == 1:
-                pass_on(g, up, unit_of(zlo, ym, core))
-            if g in Y_FIRST:
-                pass_on(g, up, unit_of(zo, y, core))
-
-    def y_far(g, z):
-        for c in range(2):
-            u = unit_of(z, yo, c)
-            landed(g, u)
-            if g in Y_FIRST:
-                pass_on(g, u, unit_of(zo, y, core))
-
-    def own_plane(g):
-        relay(g, zlo)
-        if g in Y_FIRST:
-            for c in range(2):
-                u = unit_of(zlo, y, c)
-                pass_on(g, u, unit_of(zo, y, core))
-            y_far(g, zlo)
-
-    def z_arrivals(g):
-        if g in Y_FIRST:
-            return
-        for c in range(2):
-            u = unit_of(zo, y, c)
-            landed(g, u)
-            pass_on(g, u, unit_of(zlo, yp, core))
-            pass_on(g, u, unit_of(zlo, ym, core))
-
-    def other_plane(g):
-        if g not in Y_FIRST:
-            relay(g, zo)
-
-    def last_units(g):
-        if g in Y_FIRST:
-            for yy in range(4):
-                for c in range(2):
-                    landed(g, unit_of(zo, yy, c))
-        else:
-            y_far(g, zlo)
-            y_far(g, zo)
+        for g, (tile, first, rows) in enumerate(PIECES):
+            if tile != cc:
+                continue
+            for half, dst in ((1 - core, other[g]), (core, gath[g].at[row])):
+                for p in range(2):
+                    for a in range(rows):
+                        at = p * ROWS + first + a + half * HALF
+                        values = plain[pl.ds(at, NKA, stride=2 * ROWS), :]
+                        dst[p * rows + a] = values.astype(BF)
+                if dst is other[g]:
+                    remote(
+                        other[g], gath[g].at[row], g_s.at[g], g_r.at[g, row], (ka, mate)
+                    ).start()
+            pass_on(g, 0, 0, 0)
+
+    def unit_at(plane, dy, r):
+        return unit_of((zlo + plane) % 2, (y + dy + 4) % 4, (core + r) % 2)
+
+    def pass_on(g, plane, dy, r):
+        u = unit_at(plane, dy, r)
+        y_first = g in Y_FIRST
+        to = []
+        if plane == 0 or not y_first:
+            if dy == 0 or (dy == -1 and r == 0):
+                to.append(unit_of(zlo, yp, core))
+            if dy == 0 or (dy == 1 and r == 1):
+                to.append(unit_of(zlo, ym, core))
+        if plane == 0 and (y_first or dy == 0):
+            to.append(unit_of(zo, y, core))
+        for t in to:
+            remote(gath[g].at[u], gath[g].at[u], g_s.at[g], g_r.at[g, u], (ka, t)).start()
+
+    def landed(g, plane, dy, r):
+        u = unit_at(plane, dy, r)
+        wait_bytes(gath[g].at[u], g_r.at[g, u])
 
     def build_factors():
         wait_bytes(mixr.at[pl.ds(0, NROW - 1)], m_r)
@@ -286,33 +250,31 @@
     scale = 1.0 / nk
 
     def transform(g):
-        last_units(g)
-        cc = g // PARTS
-        first = (g % PARTS) * SUB
+        cc, first, rows = PIECES[g]
 
         def one(i, carry):
             a = 2 * i
-            re0 = gath[g, :, a].reshape(nk, 128)
-            re1 = gath[g, :, a + 1].reshape(nk, 128)
-            im0 = gath[g, :, SUB + a].reshape(nk, 128)
-            im1 = gath[g, :, SUB + a + 1].reshape(nk, 128)
-            x = jnp.concatenate(
+            re0 = gath[g][:, a].reshape(nk, 128)
+            re1 = gath[g][:, a + 1].reshape(nk, 128)
+            im0 = gath[g][:, rows + a].reshape(nk, 128)
+            im1 = gath[g][:, rows + a + 1].reshape(nk, 128)
+            both = jnp.concatenate(
                 [jnp.concatenate([re0, re1], 1), jnp.concatenate([im0, im1], 1)], 0
             )
-            y_all = jnp.dot(lmat[...], x, preferred_element_type=F32) * scale
+            product = jnp.dot(lmat[...], both, preferred_element_type=F32) * scale
             for b in range(2):
-                v = y_all[:, b * 128 : b * 128 + 128]
+                v = product[:, b * 128 : b * 128 + 128]
                 for p in range(2):
                     place(cc, p, core * HALF + first + a + b, v[p * r_dev : (p + 1) * r_dev])
-                    stage_l[g, p, a + b] = v[(2 + p) * r_dev : (3 + p) * r_dev].astype(BF)
+                    stage_l[g][p, a + b] = v[(2 + p) * r_dev : (3 + p) * r_dev].astype(BF)
                 vp = v[4 * r_dev : 4 * r_dev + 8] + v[4 * r_dev + 8 :]
                 place_path(cc, core * HALF + first + a + b, vp[:4])
-                stage_p[g, a + b] = vp
+                stage_p[g][a + b] = vp
             return carry
 
-        lax.fori_loop(0, SUB // 2, one, 0)
-        remote(stage_l.at[g], from_l.at[g], o_s.at[g], o_r.at[g], (ka, mate)).start()
-        remote(stage_p.at[g], from_p.at[g], op_s.at[g], op_r.at[g], (ka, mate)).start()
+        lax.fori_loop(0, rows // 2, one, 0)
+        remote(stage_l[g], from_l[g], o_s.at[g], o_r.at[g], (ka, mate)).start()
+        remote(stage_p[g], from_p[g], op_s.at[g], op_r.at[g], (ka, mate)).start()
 
     def place(cc, p, a, value):
         rows_f[cc, p, pl.ds(a, r_dev, stride=ROWS), :] = value
@@ -322,18 +284,18 @@
             rows_p[cc, p, pl.ds(a, 2, stride=ROWS), :] = value[2 * p : 2 * p + 2]
 
     def from_other_core(g):
-        cc = g // PARTS
-        first = (1 - core) * HALF + (g % PARTS) * SUB
-        wait_bytes(stage_l.at[g], o_r.at[g])
-        wait_bytes(stage_p.at[g], op_r.at[g])
+        cc, first, rows = PIECES[g]
+        start = (1 - core) * HALF + first
+        wait_bytes(stage_l[g], o_r.at[g])
+        wait_bytes(stage_p[g], op_r.at[g])
 
         def one(a, carry):
             for p in range(2):
-                place(cc, p, first + a, from_l[g, p, a].astype(F32))
-            place_path(cc, first + a, from_p[g, a, 4:])
+                place(cc, p, start + a, from_l[g][p, a].astype(F32))
+            place_path(cc, start + a, from_p[g][a, 4:])
             return carry
 
-        lax.fori_loop(0, SUB, one, 0)
+        lax.fori_loop(0, rows, one, 0)
 
     def write_out(cc):
         step = 8
@@ -352,58 +314,42 @@
             for q in range(2):
                 out_p[q, :, cols] = rows_p[cc, p, q * ROWS : (q + 1) * ROWS, :]
 
-    transpose(0)
-    from_mate(0)
-    from_mate(1)
-    spread(2)
-    own_plane(0)
-    own_plane(1)
-    transpose(1)
-    from_mate(2)
-    from_mate(3)
-    z_arrivals(0)
-    z_arrivals(1)
-    other_plane(0)
-    other_plane(1)
-    transpose(2)
-    from_mate(4)
-    from_mate(5)
-    own_plane(2)
-    own_plane(3)
-    build_factors()
-    z_arrivals(2)
-    z_arrivals(3)
-    transform(0)
-    transform(1)
-    other_plane(2)
-    other_plane(3)
-    own_plane(4)
-    own_plane(5)
-    z_arrivals(4)
-    z_arrivals(5)
-    transform(2)
-    transform(3)
-    from_other_core(0)
-    from_other_core(1)
-    write_out(0)
-    other_plane(4)
-    other_plane(5)
-    from_other_core(2)
-    from_other_core(3)
-    write_out(1)
-    transform(4)
-    transform(5)
-    from_other_core(4)
-    from_other_core(5)
-    write_out(2)
+    everything = [(pn, dy, r) for pn in range(2) for dy in (0, -1, 1, 2) for r in range(2)][1:]
+    pending = {g: list(everything) for g in range(CHUNKS)}
+    left = {cc: sum(t == cc for t, _, _ in PIECES) for cc in range(TILES)}
+
+    def finish(g):
+        from_other_core(g)
+        left[PIECES[g][0]] -= 1
+        if left[PIECES[g][0]] == 0:
+            write_out(PIECES[g][0])
+
+    last = None
+    for what, g, *unit in ORDER:
+        if what == 0:
+            take_tile(g)
+        elif what == 1:
+            landed(g, *unit)
+            pending[g].remove(tuple(unit))
+            pass_on(g, *unit)
+        else:
+            if last is None:
+                build_factors()
+            for rest in pending[g]:
+                landed(g, *rest)
+            transform(g)
+            if last is not None:
+                finish(last)
+            last = g
+    finish(last)
 
     for cc in range(TILES):
         wait_bytes(send.at[cc, pl.ds(0, NKA - 1)], a2a_s.at[cc])
     wait_bytes(mixr.at[pl.ds(0, NROW - 1)], m_s)
     for g in range(CHUNKS):
-        wait_bytes(gath.at[g, pl.ds(0, NROW - 1)], g_s.at[g])
-        wait_bytes(stage_l.at[g], o_s.at[g])
-        wait_bytes(stage_p.at[g], op_s.at[g])
+        wait_bytes(gath[g].at[pl.ds(0, NROW - 1)], g_s.at[g])
+        wait_bytes(stage_l[g], o_s.at[g])
+        wait_bytes(stage_p[g], op_s.at[g])
 
 
 def local(gauge, energies, kmesh, lattice, degeneracy, path):
@@ -414,6 +360,7 @@
     vmem = pl.BlockSpec(memory_space=pltpu.VMEM)
     dma = pltpu.SemaphoreType.DMA
     hbm = pl.BlockSpec(memory_space=pltpu.HBM)
+    rows = [n for _, _, n in PIECES]
     return pl.pallas_call(
         kernel,
         out_shape=(
@@ -435,16 +382,16 @@
             pltpu.VMEM((TILES, NKA, 2 * ROWS, 128), BF),
             pltpu.VMEM((TILES, NKA, 2 * ROWS, 128), BF),
             pltpu.VMEM((NKA * 2 * ROWS, 128), F32),
-            pltpu.VMEM((CHUNKS, UNIT, NKA, 128), BF),
-            pltpu.VMEM((CHUNKS, NROW, UNIT, NKA, 128), BF),
+            [pltpu.VMEM((2 * n, NKA, 128), BF) for n in rows],
+            [pltpu.VMEM((NROW, 2 * n, NKA, 128), BF) for n in rows],
             pltpu.VMEM((4 * r_dev + 16, 2 * nk), BF),
             pltpu.VMEM((2, r_dev, 2 * nk), BF),
             pltpu.VMEM((NROW // 2, 8, nk), F32),
             pltpu.VMEM((NROW, 8, nk), F32),
-            pltpu.VMEM((CHUNKS, 2, SUB, r_dev, 128), BF),
-            pltpu.VMEM((CHUNKS, SUB, 8, 128), F32),
-            pltpu.VMEM((CHUNKS, 2, SUB, r_dev, 128), BF),
-            pltpu.VMEM((CHUNKS, SUB, 8, 128), F32),
+            [pltpu.VMEM((2, n, r_dev, 128), BF) for n in rows],
+            [pltpu.VMEM((n, 8, 128), F32) for n in rows],
+            [pltpu.VMEM((2, n, r_dev, 128), BF) for n in rows],
+            [pltpu.VMEM((n, 8, 128), F32) for n in rows],
             pltpu.VMEM((TILES, 2, r_dev * ROWS, 128), F32),
             pltpu.VMEM((TILES, 2, path_dev * ROWS, 128), F32),
             pltpu.VMEM((4, path_dev, 2 * nk), F32),
@@ -464,7 +411,12 @@
         compiler_params=pltpu.CompilerParams(
             collective_id=0, has_side_effects=True, vmem_limit_bytes=48 << 20
         ),
-    )(*[pltpu.with_memory_space_constraint(v, pltpu.HBM) for v in (gauge[0], energies, kmesh, lattice, degeneracy[None, :], path)])
+    )(
+        *[
+            pltpu.with_memory_space_constraint(v, pltpu.HBM)
+            for v in (gauge[0], energies, kmesh, lattice, degeneracy[None, :], path)
+        ]
+    )
 
 
 def solution(mesh):

time: 68.2 us -> 59.9 us (0.88)
  Pallas kernels: 65.3 us -> 57.1 us
    pallas_call x1, Pallas kernels: 65.3 us -> 57.1 us  [local(): pl.pallas_call(kernel, out_shape=(jax.ShapeDtypeStruct((r_dev, ROWS, 2 *...]
where the time goes in v3:
time: 59.9 us; the launch traced here: 59.8 us
  Pallas kernels  57.1 us (95%)
  local copies, waits for them, and re-layouts  2.07 us (3%)
  between operations  0.64 us (1%)
    pallas_call x1, Pallas kernels, local(): pl.pallas_call(kernel, out_shape=(jax.ShapeDtypeStruct((r_dev, ROWS, 2 *...  57.1 us
    unnamed x2, local copies, waits for them, and re-layouts  2.07 us

profile of v3, /device:TPU:1, one launch (start us, length us, event | category | flops | bytes accessed | tf_op | source)
XLA Modules:
  0.0 59.8 jit_solution(15897774478142279856)
XLA Ops:
  0.6 57.1 %shard_map.77 = (bf16[64,24,768]{2,1,0:T(8,128)(2,1)S(1)}, f32[2,24,768]{2,1,0:T(8,128)S(1)}) custom-call(bf16[2,384,384]{2,1,0:T(8,128)(2,1)} %bitcast.2, f32[1,384]{1,0:T(1,128)} %energies_h.1, s32[3,256]{1,0:T(4,128)} %kmesh_h.1, s32[3,64]{1,0:T(4,128)} %lattice_h.1, s32[1,64]{1,0:T(1,128)} %bitcast.3, s32[3,32]{1,0:T(4,128)} %path_h.1), custom_call_target="tpu_custom_call" | custom-call | tf_op jit(solution)/shard_map/pallas_call | solution.py:364
  57.7 1.4 %copy.10 = bf16[64,24,768]{2,1,0:T(8,128)(2,1)} copy(bf16[64,24,768]{2,1,0:T(8,128)(2,1)S(1)} %get-tuple-element.4) | data formatting | bytes 4718592
  59.1 0.7 %copy.11 = f32[2,24,768]{2,1,0:T(8,128)} copy(f32[2,24,768]{2,1,0:T(8,128)S(1)} %get-tuple-element.5) | data formatting | bytes 294912

commit v4 on v3

--- a/solution.py
+++ b/solution.py
@@ -1,4 +1,3 @@
-import functools
 import math
 
 import jax
@@ -15,16 +14,19 @@
 ROWS = 24
 TILES = 3
 HALF = ROWS // 2
-PIECES = ((0, 0, 12), (1, 0, 6), (1, 6, 6), (2, 0, 4), (2, 4, 4), (2, 8, 4))
-Y_FIRST = (1, 2, 3,)
+BLOCKS = ((0, 0, 4), (0, 4, 4), (0, 8, 4), (1, 0, 12), (2, 0, 12))
+PIECES = ((0, 0, 4), (0, 4, 4), (0, 8, 4), (1, 0, 6), (1, 6, 6), (2, 0, 6), (2, 6, 6))
+Y_FIRST = (1, 4, 5,)
 ORDER = (
-    (0,0), (1,0,0,0,1), (0,1), (1,0,0,-1,0), (1,0,1,0,0), (1,1,0,0,1), (1,2,0,0,1), (1,0,0,1,1),
-    (1,0,1,0,1), (1,1,0,-1,0), (1,1,0,1,0), (0,2), (1,2,0,-1,0), (1,2,0,1,0), (1,3,0,0,1),
-    (1,4,0,0,1), (1,5,0,0,1), (1,1,0,1,1), (1,0,1,-1,0), (1,2,0,1,1), (1,1,0,-1,1), (1,4,1,0,0),
-    (1,5,1,0,0), (1,2,0,-1,1), (1,0,1,1,1), (1,3,0,1,0), (1,1,0,2,0), (1,4,1,0,1), (1,3,0,-1,0),
-    (1,5,1,0,1), (1,4,0,-1,0), (1,3,0,1,1), (1,5,0,-1,0), (1,4,0,1,1), (1,2,0,2,0), (1,5,0,1,1),
-    (1,3,0,-1,1), (1,1,0,2,1), (1,2,0,2,1), (1,4,1,-1,0), (1,5,1,-1,0), (2,0), (1,4,1,1,1),
-    (1,3,0,2,0), (1,5,1,1,1), (1,3,0,2,1), (2,1), (2,2), (2,4), (2,5), (2,3),
+    (0,0), (0,1), (1,0,0,0,1), (1,0,0,-1,0), (0,2), (1,1,0,0,1), (1,0,1,0,0), (1,1,0,-1,0),
+    (1,1,0,1,0), (1,2,0,0,1), (1,0,0,1,1), (1,0,1,0,1), (1,2,1,0,0), (1,2,0,-1,0), (1,1,0,1,1),
+    (1,1,0,-1,1), (0,3), (1,0,1,-1,0), (1,2,0,1,1), (1,1,0,2,0), (1,2,1,0,1), (1,3,0,0,1),
+    (1,4,0,0,1), (1,0,1,1,1), (1,2,1,-1,0), (1,1,0,2,1), (1,3,1,0,0), (0,4), (1,3,0,-1,0),
+    (1,4,0,1,0), (1,5,0,0,1), (1,6,0,0,1), (1,4,0,-1,0), (1,3,1,0,1), (1,2,1,1,1), (1,3,0,1,1),
+    (2,1), (1,4,0,1,1), (1,4,0,-1,1), (2,0), (1,6,1,0,0), (1,3,1,-1,0), (1,5,0,1,0),
+    (1,5,0,-1,0), (1,6,0,-1,0), (1,6,1,0,1), (1,5,0,1,1), (1,6,0,1,1), (1,5,0,-1,1),
+    (1,3,1,1,1), (2,2), (1,4,0,2,0), (1,4,0,2,1), (1,6,1,-1,0), (1,6,1,1,1), (1,5,0,2,0),
+    (1,5,0,2,1), (2,4), (2,3), (2,6), (2,5),
 )
 CHUNKS = len(PIECES)
 
@@ -113,17 +115,27 @@
         )
         h = jnp.dot(at_ref[...], rhs, preferred_element_type=F32)
         for j in range(NKA):
-            both = jnp.concatenate(
-                [h[j * ROWS : (j + 1) * ROWS, :128], h[j * ROWS : (j + 1) * ROWS, 128:]], 0
-            )
-            send[cc, j] = both.astype(BF)
+            groups = [
+                h[j * ROWS + t * 8 : j * ROWS + t * 8 + 8, p * 128 : p * 128 + 128]
+                for t in range(ROWS // 8)
+                for p in range(2)
+            ]
+            send[cc, j] = jnp.concatenate(groups, 0).astype(BF)
+
+    def lines_of(i):
+        return pl.ds(BLOCKS[i][1] * 4, BLOCKS[i][2] * 4)
 
     def spread(cc):
-        for dx, d in peers:
-            to = place_of(x + dx, (z + turn * (0, 1, -2, 3)[d] + 8) % 8)
-            remote(
-                send.at[cc, to[0]], arrived.at[cc, x * 4 + d], a2a_s.at[cc], a2a_r.at[cc], to
-            ).start()
+        for i, (tile, _, _) in enumerate(BLOCKS):
+            if tile != cc:
+                continue
+            lines = lines_of(i)
+            for dx, d in peers:
+                to = place_of(x + dx, (z + turn * (0, 1, -2, 3)[d] + 8) % 8)
+                remote(
+                    send.at[cc, to[0], lines], arrived.at[cc, x * 4 + d, lines],
+                    a2a_s.at[i], a2a_r.at[i], to,
+                ).start()
         arrived[cc, pl.ds(x * 4, 1)] = send[cc, pl.ds(ka, 1)]
 
     rotate(0)
@@ -181,17 +193,21 @@
         remote(mixp.at[to // 2], mixr.at[row], m_s, m_r, (ka, to)).start()
     mixr[pl.ds(row, 1)] = mixp[pl.ds(row // 2, 1)]
 
-    def take_tile(cc):
-        wait_bytes(arrived.at[cc, pl.ds(0, NKA - 1)], a2a_r.at[cc])
-        plain[...] = arrived[cc].reshape(NKA * 2 * ROWS, 128).astype(F32)
+    def take_block(i):
+        cc, start, count = BLOCKS[i]
+        lines = count * 4
+        wait_bytes(arrived.at[cc, pl.ds(0, NKA - 1), lines_of(i)], a2a_r.at[i])
+        block = arrived[cc, :, lines_of(i)]
+        plain[: NKA * lines] = block.reshape(NKA * lines, 128).astype(F32)
         for g, (tile, first, rows) in enumerate(PIECES):
-            if tile != cc:
+            if tile != cc or not start <= first < start + count:
                 continue
             for half, dst in ((1 - core, other[g]), (core, gath[g].at[row])):
                 for p in range(2):
                     for a in range(rows):
-                        at = p * ROWS + first + a + half * HALF
-                        values = plain[pl.ds(at, NKA, stride=2 * ROWS), :]
+                        at = first + a - start
+                        at = (at // 4) * 16 + p * 8 + at % 4 + half * 4
+                        values = plain[pl.ds(at, NKA, stride=lines), :]
                         dst[p * rows + a] = values.astype(BF)
                 if dst is other[g]:
                     remote(
@@ -265,10 +281,10 @@
             for b in range(2):
                 v = product[:, b * 128 : b * 128 + 128]
                 for p in range(2):
-                    place(cc, p, core * HALF + first + a + b, v[p * r_dev : (p + 1) * r_dev])
+                    place(cc, p, core, first + a + b, v[p * r_dev : (p + 1) * r_dev])
                     stage_l[g][p, a + b] = v[(2 + p) * r_dev : (3 + p) * r_dev].astype(BF)
                 vp = v[4 * r_dev : 4 * r_dev + 8] + v[4 * r_dev + 8 :]
-                place_path(cc, core * HALF + first + a + b, vp[:4])
+                place_path(cc, core, first + a + b, vp[:4])
                 stage_p[g][a + b] = vp
             return carry
 
@@ -276,23 +292,25 @@
         remote(stage_l[g], from_l[g], o_s.at[g], o_r.at[g], (ka, mate)).start()
         remote(stage_p[g], from_p[g], op_s.at[g], op_r.at[g], (ka, mate)).start()
 
-    def place(cc, p, a, value):
-        rows_f[cc, p, pl.ds(a, r_dev, stride=ROWS), :] = value
-
-    def place_path(cc, a, value):
+    def row_at(half, a):
+        return (a // 4) * 8 + half * 4 + a % 4
+
+    def place(cc, p, half, a, value):
+        rows_f[cc, p, pl.ds(row_at(half, a), r_dev, stride=ROWS), :] = value
+
+    def place_path(cc, half, a, value):
         for p in range(2):
-            rows_p[cc, p, pl.ds(a, 2, stride=ROWS), :] = value[2 * p : 2 * p + 2]
+            rows_p[cc, p, pl.ds(row_at(half, a), 2, stride=ROWS), :] = value[2 * p : 2 * p + 2]
 
     def from_other_core(g):
         cc, first, rows = PIECES[g]
-        start = (1 - core) * HALF + first
         wait_bytes(stage_l[g], o_r.at[g])
         wait_bytes(stage_p[g], op_r.at[g])
 
         def one(a, carry):
             for p in range(2):
-                place(cc, p, start + a, from_l[g][p, a].astype(F32))
-            place_path(cc, start + a, from_p[g][a, 4:])
+                place(cc, p, 1 - core, first + a, from_l[g][p, a].astype(F32))
+            place_path(cc, 1 - core, first + a, from_p[g][a, 4:])
             return carry
 
         lax.fori_loop(0, rows, one, 0)
@@ -327,7 +345,7 @@
     last = None
     for what, g, *unit in ORDER:
         if what == 0:
-            take_tile(g)
+            take_block(g)
         elif what == 1:
             landed(g, *unit)
             pending[g].remove(tuple(unit))
@@ -343,8 +361,8 @@
             last = g
     finish(last)
 
-    for cc in range(TILES):
-        wait_bytes(send.at[cc, pl.ds(0, NKA - 1)], a2a_s.at[cc])
+    for i, (cc, _, _) in enumerate(BLOCKS):
+        wait_bytes(send.at[cc, pl.ds(0, NKA - 1), lines_of(i)], a2a_s.at[i])
     wait_bytes(mixr.at[pl.ds(0, NROW - 1)], m_s)
     for g in range(CHUNKS):
         wait_bytes(gath[g].at[pl.ds(0, NROW - 1)], g_s.at[g])
@@ -395,8 +413,8 @@
             pltpu.VMEM((TILES, 2, r_dev * ROWS, 128), F32),
             pltpu.VMEM((TILES, 2, path_dev * ROWS, 128), F32),
             pltpu.VMEM((4, path_dev, 2 * nk), F32),
-            dma((TILES,)),
-            dma((TILES,)),
+            dma((len(BLOCKS),)),
+            dma((len(BLOCKS),)),
             dma((CHUNKS,)),
             dma((CHUNKS, NROW)),
             dma,

time: 59.9 us -> 59.4 us (level)
  no operation moved by 1% of the time
where the time goes in v4:
time: 59.4 us; the launch traced here: 59.3 us
  Pallas kernels  56.6 us (95%)
  local copies, waits for them, and re-layouts  2.07 us (3%)
  between operations  0.64 us (1%)
    pallas_call x1, Pallas kernels, local(): pl.pallas_call(kernel, out_shape=(jax.ShapeDtypeStruct((r_dev, ROWS, 2 *...  56.6 us
    unnamed x2, local copies, waits for them, and re-layouts  2.07 us

profile of v4, /device:TPU:1, one launch (start us, length us, event | category | flops | bytes accessed | tf_op | source)
XLA Modules:
  0.0 59.3 jit_solution(5115383246869111806)
XLA Ops:
  0.6 56.6 %shard_map.77 = (bf16[64,24,768]{2,1,0:T(8,128)(2,1)S(1)}, f32[2,24,768]{2,1,0:T(8,128)S(1)}) custom-call(bf16[2,384,384]{2,1,0:T(8,128)(2,1)} %bitcast.2, f32[1,384]{1,0:T(1,128)} %energies_h.1, s32[3,256]{1,0:T(4,128)} %kmesh_h.1, s32[3,64]{1,0:T(4,128)} %lattice_h.1, s32[1,64]{1,0:T(1,128)} %bitcast.3, s32[3,32]{1,0:T(4,128)} %path_h.1), custom_call_target="tpu_custom_call" | custom-call | tf_op jit(solution)/shard_map/pallas_call | solution.py:382
  57.2 1.4 %copy.10 = bf16[64,24,768]{2,1,0:T(8,128)(2,1)} copy(bf16[64,24,768]{2,1,0:T(8,128)(2,1)S(1)} %get-tuple-element.4) | data formatting | bytes 4718592
  58.6 0.7 %copy.11 = f32[2,24,768]{2,1,0:T(8,128)} copy(f32[2,24,768]{2,1,0:T(8,128)S(1)} %get-tuple-element.5) | data formatting | bytes 294912

commit v5 on v4

--- a/solution.py
+++ b/solution.py
@@ -399,7 +399,7 @@
             pltpu.VMEM((2, w, w), BF),
             pltpu.VMEM((TILES, NKA, 2 * ROWS, 128), BF),
             pltpu.VMEM((TILES, NKA, 2 * ROWS, 128), BF),
-            pltpu.VMEM((NKA * 2 * ROWS, 128), F32),
+            pltpu.VMEM(((NKA + 1) * 2 * ROWS, 128), F32),
             [pltpu.VMEM((2 * n, NKA, 128), BF) for n in rows],
             [pltpu.VMEM((NROW, 2 * n, NKA, 128), BF) for n in rows],
             pltpu.VMEM((4 * r_dev + 16, 2 * nk), BF),
@@ -410,8 +410,8 @@
             [pltpu.VMEM((n, 8, 128), F32) for n in rows],
             [pltpu.VMEM((2, n, r_dev, 128), BF) for n in rows],
             [pltpu.VMEM((n, 8, 128), F32) for n in rows],
-            pltpu.VMEM((TILES, 2, r_dev * ROWS, 128), F32),
-            pltpu.VMEM((TILES, 2, path_dev * ROWS, 128), F32),
+            pltpu.VMEM((TILES, 2, (r_dev + 1) * ROWS, 128), F32),
+            pltpu.VMEM((TILES, 2, (path_dev + 1) * ROWS, 128), F32),
             pltpu.VMEM((4, path_dev, 2 * nk), F32),
             dma((len(BLOCKS),)),
             dma((len(BLOCKS),)),

time: 59.4 us -> 59.4 us (level)
  no operation moved by 1% of the time
where the time goes in v5:
time: 59.4 us; the launch traced here: 59.3 us
  Pallas kernels  56.6 us (95%)
  local copies, waits for them, and re-layouts  2.07 us (3%)
  between operations  0.64 us (1%)
    pallas_call x1, Pallas kernels, local(): pl.pallas_call(kernel, out_shape=(jax.ShapeDtypeStruct((r_dev, ROWS, 2 *...  56.6 us
    unnamed x2, local copies, waits for them, and re-layouts  2.07 us

profile of v5, /device:TPU:1, one launch (start us, length us, event | category | flops | bytes accessed | tf_op | source)
XLA Modules:
  0.0 59.3 jit_solution(5363802834031058488)
XLA Ops:
  0.6 56.6 %shard_map.77 = (bf16[64,24,768]{2,1,0:T(8,128)(2,1)S(1)}, f32[2,24,768]{2,1,0:T(8,128)S(1)}) custom-call(bf16[2,384,384]{2,1,0:T(8,128)(2,1)} %bitcast.2, f32[1,384]{1,0:T(1,128)} %energies_h.1, s32[3,256]{1,0:T(4,128)} %kmesh_h.1, s32[3,64]{1,0:T(4,128)} %lattice_h.1, s32[1,64]{1,0:T(1,128)} %bitcast.3, s32[3,32]{1,0:T(4,128)} %path_h.1), custom_call_target="tpu_custom_call" | custom-call | tf_op jit(solution)/shard_map/pallas_call | solution.py:382
  57.2 1.4 %copy.10 = bf16[64,24,768]{2,1,0:T(8,128)(2,1)} copy(bf16[64,24,768]{2,1,0:T(8,128)(2,1)S(1)} %get-tuple-element.4) | data formatting | bytes 4718592
  58.6 0.7 %copy.11 = f32[2,24,768]{2,1,0:T(8,128)} copy(f32[2,24,768]{2,1,0:T(8,128)S(1)} %get-tuple-element.5) | data formatting | bytes 294912
